TPU v7x, 32 devices: a whole 2x2x4 slice. The times are simulated.
32 devices in a mesh: ctx: 16 (over z, y, core), head: 2 (over x).
Axes of the slice: x: 2, y: 2, z: 4, core: 2. Of those that a mesh axis runs over, the one named last changes fastest.
Arguments:
- fine_query: bfloat16 [4096, 4096], P('ctx', 'head'), may hold values from -181 to 181
- fine_memory: bfloat16 [2, 4096, 1024], P(None, 'ctx', 'head'), may hold values from -6.5 to 6.5
- coarse_query: bfloat16 [2048, 4096], P('ctx', 'head'), may hold values from -181 to 181
- coarse_memory: bfloat16 [2, 2048, 1024], P(None, 'ctx', 'head'), may hold values from -6.5 to 6.5
- coarse_scale: int32 [2048], P('ctx'), may hold values from 0 to 7, never falling along the last dimension, each value on 1 to 512 neighbouring positions
- out_weight: bfloat16 [4096, 4096], P('head'), may hold values from -0.09375 to 0.09375
Outputs:
- fine_mixed: bfloat16 [4096, 4096], P(('ctx', 'head'))
- coarse_mixed: bfloat16 [2048, 4096], P(('ctx', 'head'))
Inputs may be any that keep to these rules, and one draw needn't show every extreme that they name: `coarse_scale`: never falls along the coarse tokens.
All inputs are finite; a program needn't handle non-finite values.
Results may differ from a plain program's by a relative error of at most 0.014.
Values may be sent and summed in bfloat16 or wider, within the bound.
A program may use at most 128 MiB of HBM per device.

v0:
```python
import math
import jax
import jax.numpy as jnp
from jax import lax
from jax.sharding import PartitionSpec as P

HD = 128
masked_score = -1e30


def attend_block(running, grouped, key_block, value_block, allowed, factor):
    running_max, running_sum, weighted = running
    scores = (
        jnp.einsum("rkgd,pkd->kgrp", grouped, key_block, preferred_element_type=jnp.float32)
        * factor
    )
    if allowed is not None:
        scores = jnp.where(allowed[None, None], scores, masked_score)
    new_max = jnp.maximum(running_max, jnp.max(scores, axis=-1))
    rescale = jnp.exp(running_max - new_max)
    shifted = jnp.exp(scores - new_max[..., None])
    running_sum = running_sum * rescale + jnp.sum(shifted, axis=-1)
    weighted = weighted * rescale[..., None] + jnp.einsum(
        "kgrp,pkd->kgrd",
        shifted.astype(jnp.bfloat16),
        value_block,
        preferred_element_type=jnp.float32,
    )
    return (new_max, running_sum, weighted)


def fold_keys(running, grouped, kv_piece, key_level, query_level, factor):
    length = kv_piece.shape[1]
    span_rows = math.gcd(length, 1024)
    block_count = length // span_rows
    groups = grouped.shape[1]
    key_blocks = kv_piece[0].reshape(block_count, span_rows, groups, -1)
    value_blocks = kv_piece[1].reshape(block_count, span_rows, groups, -1)
    if key_level is None:

        def advance(state, pieces):
            return (attend_block(state, grouped, pieces[0], pieces[1], None, factor), None)

        result, unused = lax.scan(advance, running, (key_blocks, value_blocks))
    else:
        level_blocks = key_level.reshape(block_count, span_rows)

        def advance(state, pieces):
            allowed = pieces[2][None, :] <= query_level[:, None]
            return (attend_block(state, grouped, pieces[0], pieces[1], allowed, factor), None)

        result, unused = lax.scan(advance, running, (key_blocks, value_blocks, level_blocks))
    return result


def mix_rows(attention, out_weight):
    return jnp.dot(attention, out_weight, preferred_element_type=jnp.float32)


def per_device(fine_query, fine_memory, coarse_query, coarse_memory, coarse_scale, out_weight):
    factor = HD ** (-0.5)
    groups = fine_memory.shape[2] // HD
    ratio = fine_query.shape[1] // (groups * HD)
    fine_rows = fine_query.shape[0]
    coarse_rows = coarse_query.shape[0]

    def group_rows(query):
        return query.reshape(query.shape[0], groups, ratio, HD)

    def start_state(length):
        return (
            jnp.full((groups, ratio, length), masked_score, jnp.float32),
            jnp.zeros((groups, ratio, length), jnp.float32),
            jnp.zeros((groups, ratio, length, HD), jnp.float32),
        )

    def finish(state):
        result = state[2] / state[1][..., None]
        return result.transpose(2, 0, 1, 3).reshape(result.shape[2], -1).astype(jnp.bfloat16)

    coarse_levels = coarse_scale.astype(jnp.float32)
    fine_grouped = group_rows(fine_query)
    fine_state = fold_keys(
        start_state(fine_rows),
        fine_grouped,
        lax.all_gather(fine_memory, "ctx", axis=1, tiled=True),
        None,
        None,
        factor,
    )
    whole_memory, whole_levels = (
        lax.all_gather(coarse_memory, "ctx", axis=1, tiled=True),
        lax.all_gather(
            coarse_levels.astype(jnp.bfloat16).reshape(1, -1), "ctx", axis=1, tiled=True
        ),
    )
    fine_state = fold_keys(fine_state, fine_grouped, whole_memory, None, None, factor)
    coarse_state = fold_keys(
        start_state(coarse_rows),
        group_rows(coarse_query),
        whole_memory,
        whole_levels[0].astype(jnp.float32),
        coarse_levels,
        factor,
    )
    fine_attention = finish(fine_state)
    coarse_attention = finish(coarse_state)
    fine_mixed = lax.psum_scatter(
        mix_rows(fine_attention, out_weight).astype(jnp.bfloat16),
        "head",
        scatter_dimension=0,
        tiled=True,
    )
    coarse_mixed = lax.psum_scatter(
        mix_rows(coarse_attention, out_weight).astype(jnp.bfloat16),
        "head",
        scatter_dimension=0,
        tiled=True,
    )
    return (fine_mixed, coarse_mixed)


def solution(mesh):
    placed = (
        P("ctx", "head"),
        P(None, "ctx", "head"),
        P("ctx", "head"),
        P(None, "ctx", "head"),
        P("ctx"),
        P("head", None),
    )
    return jax.shard_map(
        per_device,
        mesh=mesh,
        in_specs=placed,
        out_specs=(P(("ctx", "head"), None), P(("ctx", "head"), None)),
        check_vma=False,
    )
```

profile of v0, /device:TPU:0, one launch (start us, length us, event | category | flops | bytes accessed | tf_op | source)
XLA Modules:
  0.0 370.5 jit_solution(7867573203565260531)
XLA Ops:
  13.3 23.1 %all-gather.1 = bf16[16,1,128]{2,1,0:T(2,128)(2,1)S(1)} all-gather(bf16[1,1,128]{2,1,0:T(2,128)(2,1)S(1)} %get-tuple-element.299), channel_id=2, replica_groups=mesh['ctx'=16,'head'=2] {'ctx'}, dimensions={0}, use_global_device_ids=true | all-gather | bytes 4352 | tf_op jit(solution)/shard_map/all_gather | solution.py:93
  40.6 22.8 %all-gather.7.cloned.1.call-done = bf16[2,2048,512]{2,1,0:T(8,128)(2,1)} async-done(((bf16[2,128,512]{2,1,0:T(8,128)(2,1)}), bf16[2,2048,512]{2,1,0:T(8,128)(2,1)}) %all-gather.7.cloned.1.call-update) | async-done | bytes 4194320 | tf_op jit(solution)/shard_map/all_gather | solution.py:92
  82.3 33.2 %while.46 = (s32[]{:T(128)}, f32[4,4,128]{2,1,0:T(4,128)S(1)}, f32[4,4,128]{2,1,0:T(4,128)S(1)}, f32[4,4,128,128]{3,2,1,0:T(8,128)}, f32[2,1024]{1,0:T(2,128)S(1...) while((s32[]{:T(128)}, f32[4,4,128]{2,1,0:T(4,128)S(1)}, ...), condition=%wide.region_12.13_spmd.clone, body=%wide.region_9.12_spmd.clone.sunk | while | flops 1097738240 | bytes 64108184 | solution.py:52
  119.4 9.5 %convolution_convert_fusion.1 = bf16[128,4096]{1,0:T(8,128)(2,1)} fusion(bf16[128,2048]{0,1:T(8,128)(2,1)S(1)} %bitcast.155, bf16[2048,4096]{1,0:T(8,128)(2,1)} %param.17), kind=kOutput, calls=%fused_computation.64 | convolution fusion | flops 2148007936 | bytes 18350080 | tf_op jit(solution)/shard_map/dot_general | solution.py:57
  129.2 9.2 %all-gather.5.cloned.1.call-done = bf16[2,4096,512]{2,1,0:T(8,128)(2,1)} async-done(((bf16[2,256,512]{2,1,0:T(8,128)(2,1)}), bf16[2,4096,512]{2,1,0:T(8,128)(2,1)}) %all-gather.5.cloned.1.call-update) | async-done | bytes 8388624 | tf_op jit(solution)/shard_map/all_gather | solution.py:86
  158.0 107.8 %while.45 = (s32[]{:T(128)}, f32[4,4,256]{2,1,0:T(4,128)S(1)}, f32[4,4,256]{2,1,0:T(4,128)S(1)}, f32[4,4,256,128]{3,2,1,0:T(8,128)S(1)}, bf16[4,1024,4,128]{3,2,...) while((s32[]{:T(128)}, f32[4,4,256]{2,1,0:T(4,128)S(1)}, ...), condition=%wide.region_3.4_spmd.clone, body=%wide.region_0.3_spmd.clone.sunk | while | flops 2182631424 | bytes 66322564 | solution.py:44
  168.2 8.7 %fusion.81 = f32[4,4,256]{2,1,0:T(4,128)S(1)} fusion(f32[4,1024,256,4]{2,1,3,0:T(8,128)} %get-tuple-element.456, f32[4,4,256]{2,1,0:T(4,128)S(1)} %select_maximum_fusion.4), kind=kLoop, calls=%fused_computation.23.clone.1 | loop fusion | flops 12578816 | bytes 16809984 | tf_op jit(solution)/shard_map/while/body/eval_jaxpr/reduce_sum | solution.py:22
  176.9 8.0 %fusion.83 = f32[4,4,256,128]{3,2,1,0:T(8,128)S(1)} fusion(f32[4,4,256,128]{3,2,1,0:T(8,128)S(1)} %get-tuple-element.485, f32[4,1024,256,4]{2,1,3,0:T(8,128)} %get-tuple-element.456, f32[4,4,256]{2,1,0:T(4,128)S(1)} %select_maximum_fusion.4, bf16[1,1024,4,128]{3,2,1,0:T(4,128)(2,1)S(1)} %copy-done.1, f32[4,4,256]{2,1,0:T(4,128)S(1)} %get-tuple-element.459, ...), kind=kOutput, calls=%fused_computation.28.clone.1 | convolution fusion | flops 1087897600 | bytes 22052864 | tf_op jit(solution)/shard_map/while/body/eval_jaxpr/kgrp,pkd->kgrd/dot_general | solution.py:23
  195.2 8.7 %fusion.81 = f32[4,4,256]{2,1,0:T(4,128)S(1)} fusion(f32[4,1024,256,4]{2,1,3,0:T(8,128)} %get-tuple-element.456, f32[4,4,256]{2,1,0:T(4,128)S(1)} %select_maximum_fusion.4), kind=kLoop, calls=%fused_computation.23.clone.1 | loop fusion | flops 12578816 | bytes 16809984 | tf_op jit(solution)/shard_map/while/body/eval_jaxpr/reduce_sum | solution.py:22
  203.9 8.0 %fusion.83 = f32[4,4,256,128]{3,2,1,0:T(8,128)S(1)} fusion(f32[4,4,256,128]{3,2,1,0:T(8,128)S(1)} %get-tuple-element.485, f32[4,1024,256,4]{2,1,3,0:T(8,128)} %get-tuple-element.456, f32[4,4,256]{2,1,0:T(4,128)S(1)} %select_maximum_fusion.4, bf16[1,1024,4,128]{3,2,1,0:T(4,128)(2,1)S(1)} %copy-done.1, f32[4,4,256]{2,1,0:T(4,128)S(1)} %get-tuple-element.459, ...), kind=kOutput, calls=%fused_computation.28.clone.1 | convolution fusion | flops 1087897600 | bytes 22052864 | tf_op jit(solution)/shard_map/while/body/eval_jaxpr/kgrp,pkd->kgrd/dot_general | solution.py:23
  215.1 7.0 %bitcast_reduce_fusion.5 = (f32[4,4,256]{2,1,0:T(4,128)S(1)}, f32[4,1024,256,4]{2,1,3,0:T(8,128)}) fusion(bf16[256,4,4,128]{3,0,2,1:T(8,128)(2,1)S(1)} %get-tuple-element.496, bf16[1,1024,4,128]{3,2,1,0:T(4,128)(2,1)S(1)} %get-tuple-element.454), kind=kOutput, calls=%fused_computation.20.clone.1 | convolution fusion | flops 1082126336 | bytes 18890752 | tf_op jit(solution)/shard_map/while/body/eval_jaxpr/rkgd,pkd->kgrp/dot_general | solution.py:14
  222.1 8.7 %fusion.81 = f32[4,4,256]{2,1,0:T(4,128)S(1)} fusion(f32[4,1024,256,4]{2,1,3,0:T(8,128)} %get-tuple-element.456, f32[4,4,256]{2,1,0:T(4,128)S(1)} %select_maximum_fusion.4), kind=kLoop, calls=%fused_computation.23.clone.1 | loop fusion | flops 12578816 | bytes 16809984 | tf_op jit(solution)/shard_map/while/body/eval_jaxpr/reduce_sum | solution.py:22
  230.8 8.0 %fusion.83 = f32[4,4,256,128]{3,2,1,0:T(8,128)S(1)} fusion(f32[4,4,256,128]{3,2,1,0:T(8,128)S(1)} %get-tuple-element.485, f32[4,1024,256,4]{2,1,3,0:T(8,128)} %get-tuple-element.456, f32[4,4,256]{2,1,0:T(4,128)S(1)} %select_maximum_fusion.4, bf16[1,1024,4,128]{3,2,1,0:T(4,128)(2,1)S(1)} %copy-done.1, f32[4,4,256]{2,1,0:T(4,128)S(1)} %get-tuple-element.459, ...), kind=kOutput, calls=%fused_computation.28.clone.1 | convolution fusion | flops 1087897600 | bytes 22052864 | tf_op jit(solution)/shard_map/while/body/eval_jaxpr/kgrp,pkd->kgrd/dot_general | solution.py:23
  249.1 8.7 %fusion.81 = f32[4,4,256]{2,1,0:T(4,128)S(1)} fusion(f32[4,1024,256,4]{2,1,3,0:T(8,128)} %get-tuple-element.456, f32[4,4,256]{2,1,0:T(4,128)S(1)} %select_maximum_fusion.4), kind=kLoop, calls=%fused_computation.23.clone.1 | loop fusion | flops 12578816 | bytes 16809984 | tf_op jit(solution)/shard_map/while/body/eval_jaxpr/reduce_sum | solution.py:22
  257.8 8.0 %fusion.83 = f32[4,4,256,128]{3,2,1,0:T(8,128)S(1)} fusion(f32[4,4,256,128]{3,2,1,0:T(8,128)S(1)} %get-tuple-element.485, f32[4,1024,256,4]{2,1,3,0:T(8,128)} %get-tuple-element.456, f32[4,4,256]{2,1,0:T(4,128)S(1)} %select_maximum_fusion.4, bf16[1,1024,4,128]{3,2,1,0:T(4,128)(2,1)S(1)} %copy-done.1, f32[4,4,256]{2,1,0:T(4,128)S(1)} %get-tuple-element.459, ...), kind=kOutput, calls=%fused_computation.28.clone.1 | convolution fusion | flops 1087897600 | bytes 22052864 | tf_op jit(solution)/shard_map/while/body/eval_jaxpr/kgrp,pkd->kgrd/dot_general | solution.py:23
  265.8 52.2 %while.44 = (s32[]{:T(128)}, f32[4,4,256]{2,1,0:T(4,128)S(1)}, f32[4,4,256]{2,1,0:T(4,128)S(1)}, f32[4,4,256,128]{3,2,1,0:T(8,128)S(1)}, bf16[2,1024,4,128]{3,1,...) while((s32[]{:T(128)}, f32[4,4,256]{2,1,0:T(4,128)S(1)}, ...), condition=%wide.region_7.8_spmd, body=%wide.region_4.7_spmd.sunk | while | flops 2182094848 | bytes 66323060 | solution.py:44
  266.0 9.3 %bitcast_reduce_fusion.4 = (f32[4,4,256]{2,1,0:T(4,128)S(1)}, f32[4,1024,256,4]{2,1,3,0:T(8,128)}) fusion(bf16[256,4,4,128]{3,0,2,1:T(8,128)(2,1)S(1)} %get-tuple-element.521, bf16[2,1024,4,128]{3,1,2,0:T(8,128)(2,1)} %get-tuple-element.520, s32[]{:T(128)} %get-tuple-element.508), kind=kOutput, calls=%fused_computation.1.clone.1 | convolution fusion | flops 1082126336 | bytes 18891264 | tf_op jit(solution)/shard_map/while/body/eval_jaxpr/rkgd,pkd->kgrp/dot_general | solution.py:14
  275.3 8.7 %fusion.78 = f32[4,4,256]{2,1,0:T(4,128)S(1)} fusion(f32[4,1024,256,4]{2,1,3,0:T(8,128)} %get-tuple-element.444, f32[4,4,256]{2,1,0:T(4,128)S(1)} %max.16), kind=kLoop, calls=%fused_computation.4.clone.1 | loop fusion | flops 12578816 | bytes 16809984 | tf_op jit(solution)/shard_map/while/body/eval_jaxpr/reduce_sum | solution.py:22
  284.1 7.9 %multiply_add_fusion.5 = f32[4,4,256,128]{3,2,1,0:T(8,128)S(1)} fusion(f32[4,4,256,128]{3,2,1,0:T(8,128)S(1)} %get-tuple-element.511, f32[4,1024,256,4]{2,1,3,0:T(8,128)} %get-tuple-element.444, f32[4,4,256]{2,1,0:T(4,128)S(1)} %max.16, bf16[2,1024,4,128]{3,1,2,0:T(8,128)(2,1)S(1)} %copy-done.2, s32[]{:T(128)} %get-tuple-element.508, ...), kind=kOutput, calls=%fused_computation.8.clone.1 | convolution fusion | flops 1087373312 | bytes 22052868 | tf_op jit(solution)/shard_map/while/body/eval_jaxpr/kgrp,pkd->kgrd/dot_general | solution.py:23
  292.0 9.3 %bitcast_reduce_fusion.4 = (f32[4,4,256]{2,1,0:T(4,128)S(1)}, f32[4,1024,256,4]{2,1,3,0:T(8,128)}) fusion(bf16[256,4,4,128]{3,0,2,1:T(8,128)(2,1)S(1)} %get-tuple-element.521, bf16[2,1024,4,128]{3,1,2,0:T(8,128)(2,1)} %get-tuple-element.520, s32[]{:T(128)} %get-tuple-element.508), kind=kOutput, calls=%fused_computation.1.clone.1 | convolution fusion | flops 1082126336 | bytes 18891264 | tf_op jit(solution)/shard_map/while/body/eval_jaxpr/rkgd,pkd->kgrp/dot_general | solution.py:14
  301.3 8.7 %fusion.78 = f32[4,4,256]{2,1,0:T(4,128)S(1)} fusion(f32[4,1024,256,4]{2,1,3,0:T(8,128)} %get-tuple-element.444, f32[4,4,256]{2,1,0:T(4,128)S(1)} %max.16), kind=kLoop, calls=%fused_computation.4.clone.1 | loop fusion | flops 12578816 | bytes 16809984 | tf_op jit(solution)/shard_map/while/body/eval_jaxpr/reduce_sum | solution.py:22
  310.0 7.9 %multiply_add_fusion.5 = f32[4,4,256,128]{3,2,1,0:T(8,128)S(1)} fusion(f32[4,4,256,128]{3,2,1,0:T(8,128)S(1)} %get-tuple-element.511, f32[4,1024,256,4]{2,1,3,0:T(8,128)} %get-tuple-element.444, f32[4,4,256]{2,1,0:T(4,128)S(1)} %max.16, bf16[2,1024,4,128]{3,1,2,0:T(8,128)(2,1)S(1)} %copy-done.2, s32[]{:T(128)} %get-tuple-element.508, ...), kind=kOutput, calls=%fused_computation.8.clone.1 | convolution fusion | flops 1087373312 | bytes 22052868 | tf_op jit(solution)/shard_map/while/body/eval_jaxpr/kgrp,pkd->kgrd/dot_general | solution.py:23
  321.6 11.6 %convolution_convert_fusion = bf16[256,4096]{1,0:T(8,128)(2,1)} fusion(bf16[256,2048]{0,1:T(8,128)(2,1)S(1)} %bitcast.153, bf16[2048,4096]{1,0:T(8,128)(2,1)} %param.17), kind=kOutput, calls=%fused_computation.63 | convolution fusion | flops 4296015872 | bytes 19922944 | tf_op jit(solution)/shard_map/dot_general | solution.py:57
  333.3 30.7 %reduce-scatter.3.cloned.1.call-done = bf16[128,4096]{1,0:T(8,128)(2,1)} async-done(((bf16[256,4096]{1,0:T(8,128)(2,1)}), bf16[128,4096]{1,0:T(8,128)(2,1)}) %reduce-scatter.3.cloned.1.call-update) | async-done | bytes 1048592 | tf_op jit(solution)/shard_map/reduce_scatter | solution.py:108
  (91 shorter events, 123.8 us)
Async XLA Ops:
  7.2 56.2 %all-gather.7.cloned.1.call-start = ((), (), s32[]{:S(2)}) async-start(), calls=%async_computation.3 | async-start | bytes 4456448 | tf_op jit(solution)/shard_map/all_gather | solution.py:92
  7.9 130.5 %all-gather.5.cloned.1.call-start = ((), (), s32[]{:S(2)}) async-start(), calls=%async_computation.2 | async-start | bytes 8912896 | tf_op jit(solution)/shard_map/all_gather | solution.py:86
  8.6 324.6 %reduce-scatter.5.cloned.1.call-start = ((), (), s32[]{:S(2)}) async-start(), calls=%async_computation.5 | async-start | bytes 1572864 | tf_op jit(solution)/shard_map/reduce_scatter | solution.py:114
  88.4 5.8 %copy-start = (f32[4,1024,128,4]{2,1,3,0:T(8,128)S(1)}, f32[4,1024,128,4]{2,1,3,0:T(8,128)}, u32[]{:S(2)}) copy-start(f32[4,1024,128,4]{2,1,3,0:T(8,128)} %get-tuple-element.470) | copy-start | bytes 25165828 | tf_op jit(solution)/shard_map/while
  104.9 5.9 %copy-start = (f32[4,1024,128,4]{2,1,3,0:T(8,128)S(1)}, f32[4,1024,128,4]{2,1,3,0:T(8,128)}, u32[]{:S(2)}) copy-start(f32[4,1024,128,4]{2,1,3,0:T(8,128)} %get-tuple-element.470) | copy-start | bytes 25165828 | tf_op jit(solution)/shard_map/while
  128.9 235.0 %reduce-scatter.3.cloned.1.call-start = ((), (), s32[]{:S(2)}) async-start(), calls=%async_computation.4 | async-start | bytes 3145728 | tf_op jit(solution)/shard_map/reduce_scatter | solution.py:108
  168.2 8.7 %copy-start.1 = (bf16[1,1024,4,128]{3,2,1,0:T(4,128)(2,1)S(1)}, bf16[1,1024,4,128]{3,2,1,0:T(4,128)(2,1)}, u32[]{:S(2)}) copy-start(bf16[1,1024,4,128]{3,2,1,0:T(4,128)(2,1)} %get-tuple-element.458) | copy-start | bytes 3145732 | tf_op jit(solution)/shard_map/while
  195.2 8.7 %copy-start.1 = (bf16[1,1024,4,128]{3,2,1,0:T(4,128)(2,1)S(1)}, bf16[1,1024,4,128]{3,2,1,0:T(4,128)(2,1)}, u32[]{:S(2)}) copy-start(bf16[1,1024,4,128]{3,2,1,0:T(4,128)(2,1)} %get-tuple-element.458) | copy-start | bytes 3145732 | tf_op jit(solution)/shard_map/while
  222.1 8.7 %copy-start.1 = (bf16[1,1024,4,128]{3,2,1,0:T(4,128)(2,1)S(1)}, bf16[1,1024,4,128]{3,2,1,0:T(4,128)(2,1)}, u32[]{:S(2)}) copy-start(bf16[1,1024,4,128]{3,2,1,0:T(4,128)(2,1)} %get-tuple-element.458) | copy-start | bytes 3145732 | tf_op jit(solution)/shard_map/while
  249.1 8.7 %copy-start.1 = (bf16[1,1024,4,128]{3,2,1,0:T(4,128)(2,1)S(1)}, bf16[1,1024,4,128]{3,2,1,0:T(4,128)(2,1)}, u32[]{:S(2)}) copy-start(bf16[1,1024,4,128]{3,2,1,0:T(4,128)(2,1)} %get-tuple-element.458) | copy-start | bytes 3145732 | tf_op jit(solution)/shard_map/while
  275.3 8.7 %copy-start.2 = (bf16[2,1024,4,128]{3,1,2,0:T(8,128)(2,1)S(1)}, bf16[2,1024,4,128]{3,1,2,0:T(8,128)(2,1)}, u32[]{:S(2)}) copy-start(bf16[2,1024,4,128]{3,1,2,0:T(8,128)(2,1)} %get-tuple-element.522) | copy-start | bytes 6291460 | tf_op jit(solution)/shard_map/while
  301.3 8.7 %copy-start.2 = (bf16[2,1024,4,128]{3,1,2,0:T(8,128)(2,1)S(1)}, bf16[2,1024,4,128]{3,1,2,0:T(8,128)(2,1)}, u32[]{:S(2)}) copy-start(bf16[2,1024,4,128]{3,1,2,0:T(8,128)(2,1)} %get-tuple-element.522) | copy-start | bytes 6291460 | tf_op jit(solution)/shard_map/while
Sparse Core Ops, SparseCore 0:
  10.2 53.1 all-gather.6
  65.5 72.8 all-gather.4
  141.2 18.9 reduce-scatter.4
  333.4 30.5 reduce-scatter.2
where the time goes:
time: 372 us; the launch traced here: 370 us
  matrix products  136 us (37%)
  other arithmetic  67.1 us (18%)
  local copies, waits for them, and re-layouts  65 us (17%)
  waiting for transfers between devices  64.2 us (17%)
  blocking collectives  23.1 us (6%)
  between operations  13.9 us (4%)
    reduce_sum x8, other arithmetic, attend_block(): running_sum = running_sum * rescale + jnp.sum(shifted, axis=-1)  62.6 us
    dot_general x8, matrix products, attend_block(): jnp.einsum('rkgd,pkd->kgrp', grouped, key_block, preferred_element_type=j...  58.3 us
    dot_general x8, matrix products, attend_block(): jnp.einsum('kgrp,pkd->kgrd', shifted.astype(jnp.bfloat16), value_block, p...  57 us
    reduce_scatter x1, waiting for transfers between devices, per_device(): lax.psum_scatter(mix_rows(fine_attention, out_weight).astype(jnp.bfloat16...  30.7 us
    all_gather x1, blocking collectives, per_device(): lax.all_gather(coarse_levels.astype(jnp.bfloat16).reshape(1, -1), 'ctx',...  23.1 us
    all_gather x1, waiting for transfers between devices, per_device(): lax.all_gather(coarse_memory, 'ctx', axis=1, tiled=True)  22.8 us
    dot_general x2, matrix products, mix_rows(): return jnp.dot(attention, out_weight, preferred_element_type=jnp.float32)  21.1 us
    dynamic_slice x4, local copies, waits for them, and re-layouts, fold_keys(): result, unused = lax.scan(advance, running, (key_blocks, value_blocks))  12.9 us
  transfers between devices with their start and end apart: 4, of which 3 were waited for; matrix products, arithmetic and copies ran while one was open for 72% of the time, Pallas kernels for 0%

commit v1 on v0

--- a/solution.py
+++ b/solution.py
@@ -6,6 +6,11 @@
 
 HD = 128
 masked_score = -1e30
+
+
+def stack_and_merge(x, axis, d):
+    blocks = lax.all_gather(x, axis)
+    return jnp.concatenate(blocks, axis=d)
 
 
 def attend_block(running, grouped, key_block, value_block, allowed, factor):
@@ -90,9 +95,7 @@
     )
     whole_memory, whole_levels = (
         lax.all_gather(coarse_memory, "ctx", axis=1, tiled=True),
-        lax.all_gather(
-            coarse_levels.astype(jnp.bfloat16).reshape(1, -1), "ctx", axis=1, tiled=True
-        ),
+        stack_and_merge(coarse_levels.astype(jnp.bfloat16).reshape(1, -1), "ctx", 1),
     )
     fine_state = fold_keys(fine_state, fine_grouped, whole_memory, None, None, factor)
     coarse_state = fold_keys(

time: 372 us -> 372 us (level)
  no operation moved by 1% of the time
where the time goes in v1:
time: 372 us; the launch traced here: 370 us
  matrix products  136 us (37%)
  other arithmetic  67.1 us (18%)
  local copies, waits for them, and re-layouts  65 us (17%)
  waiting for transfers between devices  64.2 us (17%)
  blocking collectives  23.1 us (6%)
  between operations  13.9 us (4%)
    reduce_sum x8, other arithmetic, attend_block(): running_sum = running_sum * rescale + jnp.sum(shifted, axis=-1)  62.6 us
    dot_general x8, matrix products, attend_block(): jnp.einsum('rkgd,pkd->kgrp', grouped, key_block, preferred_element_type=j...  58.3 us
    dot_general x8, matrix products, attend_block(): jnp.einsum('kgrp,pkd->kgrd', shifted.astype(jnp.bfloat16), value_block, p...  57 us
    reduce_scatter x1, waiting for transfers between devices, per_device(): lax.psum_scatter(mix_rows(fine_attention, out_weight).astype(jnp.bfloat16...  30.7 us
    all_gather x1, blocking collectives, stack_and_merge(): blocks = lax.all_gather(x, axis)  23.1 us
    all_gather x1, waiting for transfers between devices, per_device(): lax.all_gather(coarse_memory, 'ctx', axis=1, tiled=True)  22.8 us
    dot_general x2, matrix products, mix_rows(): return jnp.dot(attention, out_weight, preferred_element_type=jnp.float32)  21.1 us
    dynamic_slice x4, local copies, waits for them, and re-layouts, fold_keys(): result, unused = lax.scan(advance, running, (key_blocks, value_blocks))  12.9 us
  transfers between devices with their start and end apart: 4, of which 3 were waited for; matrix products, arithmetic and copies ran while one was open for 72% of the time, Pallas kernels for 0%

profile of v1, /device:TPU:0, one launch (start us, length us, event | category | flops | bytes accessed | tf_op | source)
XLA Modules:
  0.0 370.5 jit_solution(7867573203565260531)
XLA Ops:
  13.3 23.1 %all-gather.1 = bf16[16,1,128]{2,1,0:T(2,128)(2,1)S(1)} all-gather(bf16[1,1,128]{2,1,0:T(2,128)(2,1)S(1)} %get-tuple-element.299), channel_id=2, replica_groups=mesh['ctx'=16,'head'=2] {'ctx'}, dimensions={0}, use_global_device_ids=true | all-gather | bytes 4352 | tf_op jit(solution)/shard_map/all_gather | solution.py:12
  40.6 22.8 %all-gather.7.cloned.1.call-done = bf16[2,2048,512]{2,1,0:T(8,128)(2,1)} async-done(((bf16[2,128,512]{2,1,0:T(8,128)(2,1)}), bf16[2,2048,512]{2,1,0:T(8,128)(2,1)}) %all-gather.7.cloned.1.call-update) | async-done | bytes 4194320 | tf_op jit(solution)/shard_map/all_gather | solution.py:97
  82.3 33.2 %while.46 = (s32[]{:T(128)}, f32[4,4,128]{2,1,0:T(4,128)S(1)}, f32[4,4,128]{2,1,0:T(4,128)S(1)}, f32[4,4,128,128]{3,2,1,0:T(8,128)}, f32[2,1024]{1,0:T(2,128)S(1...) while((s32[]{:T(128)}, f32[4,4,128]{2,1,0:T(4,128)S(1)}, ...), condition=%wide.region_12.13_spmd.clone, body=%wide.region_9.12_spmd.clone.sunk | while | flops 1097738240 | bytes 64108184 | solution.py:57
  119.4 9.5 %convolution_convert_fusion.1 = bf16[128,4096]{1,0:T(8,128)(2,1)} fusion(bf16[128,2048]{0,1:T(8,128)(2,1)S(1)} %bitcast.155, bf16[2048,4096]{1,0:T(8,128)(2,1)} %param.17), kind=kOutput, calls=%fused_computation.64 | convolution fusion | flops 2148007936 | bytes 18350080 | tf_op jit(solution)/shard_map/dot_general | solution.py:62
  129.2 9.2 %all-gather.5.cloned.1.call-done = bf16[2,4096,512]{2,1,0:T(8,128)(2,1)} async-done(((bf16[2,256,512]{2,1,0:T(8,128)(2,1)}), bf16[2,4096,512]{2,1,0:T(8,128)(2,1)}) %all-gather.5.cloned.1.call-update) | async-done | bytes 8388624 | tf_op jit(solution)/shard_map/all_gather | solution.py:91
  158.0 107.8 %while.45 = (s32[]{:T(128)}, f32[4,4,256]{2,1,0:T(4,128)S(1)}, f32[4,4,256]{2,1,0:T(4,128)S(1)}, f32[4,4,256,128]{3,2,1,0:T(8,128)S(1)}, bf16[4,1024,4,128]{3,2,...) while((s32[]{:T(128)}, f32[4,4,256]{2,1,0:T(4,128)S(1)}, ...), condition=%wide.region_3.4_spmd.clone, body=%wide.region_0.3_spmd.clone.sunk | while | flops 2182631424 | bytes 66322564 | solution.py:49
  168.2 8.7 %fusion.81 = f32[4,4,256]{2,1,0:T(4,128)S(1)} fusion(f32[4,1024,256,4]{2,1,3,0:T(8,128)} %get-tuple-element.456, f32[4,4,256]{2,1,0:T(4,128)S(1)} %select_maximum_fusion.4), kind=kLoop, calls=%fused_computation.23.clone.1 | loop fusion | flops 12578816 | bytes 16809984 | tf_op jit(solution)/shard_map/while/body/eval_jaxpr/reduce_sum | solution.py:27
  176.9 8.0 %fusion.83 = f32[4,4,256,128]{3,2,1,0:T(8,128)S(1)} fusion(f32[4,4,256,128]{3,2,1,0:T(8,128)S(1)} %get-tuple-element.485, f32[4,1024,256,4]{2,1,3,0:T(8,128)} %get-tuple-element.456, f32[4,4,256]{2,1,0:T(4,128)S(1)} %select_maximum_fusion.4, bf16[1,1024,4,128]{3,2,1,0:T(4,128)(2,1)S(1)} %copy-done.1, f32[4,4,256]{2,1,0:T(4,128)S(1)} %get-tuple-element.459, ...), kind=kOutput, calls=%fused_computation.28.clone.1 | convolution fusion | flops 1087897600 | bytes 22052864 | tf_op jit(solution)/shard_map/while/body/eval_jaxpr/kgrp,pkd->kgrd/dot_general | solution.py:28
  195.2 8.7 %fusion.81 = f32[4,4,256]{2,1,0:T(4,128)S(1)} fusion(f32[4,1024,256,4]{2,1,3,0:T(8,128)} %get-tuple-element.456, f32[4,4,256]{2,1,0:T(4,128)S(1)} %select_maximum_fusion.4), kind=kLoop, calls=%fused_computation.23.clone.1 | loop fusion | flops 12578816 | bytes 16809984 | tf_op jit(solution)/shard_map/while/body/eval_jaxpr/reduce_sum | solution.py:27
  203.9 8.0 %fusion.83 = f32[4,4,256,128]{3,2,1,0:T(8,128)S(1)} fusion(f32[4,4,256,128]{3,2,1,0:T(8,128)S(1)} %get-tuple-element.485, f32[4,1024,256,4]{2,1,3,0:T(8,128)} %get-tuple-element.456, f32[4,4,256]{2,1,0:T(4,128)S(1)} %select_maximum_fusion.4, bf16[1,1024,4,128]{3,2,1,0:T(4,128)(2,1)S(1)} %copy-done.1, f32[4,4,256]{2,1,0:T(4,128)S(1)} %get-tuple-element.459, ...), kind=kOutput, calls=%fused_computation.28.clone.1 | convolution fusion | flops 1087897600 | bytes 22052864 | tf_op jit(solution)/shard_map/while/body/eval_jaxpr/kgrp,pkd->kgrd/dot_general | solution.py:28
  215.1 7.0 %bitcast_reduce_fusion.5 = (f32[4,4,256]{2,1,0:T(4,128)S(1)}, f32[4,1024,256,4]{2,1,3,0:T(8,128)}) fusion(bf16[256,4,4,128]{3,0,2,1:T(8,128)(2,1)S(1)} %get-tuple-element.496, bf16[1,1024,4,128]{3,2,1,0:T(4,128)(2,1)S(1)} %get-tuple-element.454), kind=kOutput, calls=%fused_computation.20.clone.1 | convolution fusion | flops 1082126336 | bytes 18890752 | tf_op jit(solution)/shard_map/while/body/eval_jaxpr/rkgd,pkd->kgrp/dot_general | solution.py:19
  222.1 8.7 %fusion.81 = f32[4,4,256]{2,1,0:T(4,128)S(1)} fusion(f32[4,1024,256,4]{2,1,3,0:T(8,128)} %get-tuple-element.456, f32[4,4,256]{2,1,0:T(4,128)S(1)} %select_maximum_fusion.4), kind=kLoop, calls=%fused_computation.23.clone.1 | loop fusion | flops 12578816 | bytes 16809984 | tf_op jit(solution)/shard_map/while/body/eval_jaxpr/reduce_sum | solution.py:27
  230.8 8.0 %fusion.83 = f32[4,4,256,128]{3,2,1,0:T(8,128)S(1)} fusion(f32[4,4,256,128]{3,2,1,0:T(8,128)S(1)} %get-tuple-element.485, f32[4,1024,256,4]{2,1,3,0:T(8,128)} %get-tuple-element.456, f32[4,4,256]{2,1,0:T(4,128)S(1)} %select_maximum_fusion.4, bf16[1,1024,4,128]{3,2,1,0:T(4,128)(2,1)S(1)} %copy-done.1, f32[4,4,256]{2,1,0:T(4,128)S(1)} %get-tuple-element.459, ...), kind=kOutput, calls=%fused_computation.28.clone.1 | convolution fusion | flops 1087897600 | bytes 22052864 | tf_op jit(solution)/shard_map/while/body/eval_jaxpr/kgrp,pkd->kgrd/dot_general | solution.py:28
  249.1 8.7 %fusion.81 = f32[4,4,256]{2,1,0:T(4,128)S(1)} fusion(f32[4,1024,256,4]{2,1,3,0:T(8,128)} %get-tuple-element.456, f32[4,4,256]{2,1,0:T(4,128)S(1)} %select_maximum_fusion.4), kind=kLoop, calls=%fused_computation.23.clone.1 | loop fusion | flops 12578816 | bytes 16809984 | tf_op jit(solution)/shard_map/while/body/eval_jaxpr/reduce_sum | solution.py:27
  257.8 8.0 %fusion.83 = f32[4,4,256,128]{3,2,1,0:T(8,128)S(1)} fusion(f32[4,4,256,128]{3,2,1,0:T(8,128)S(1)} %get-tuple-element.485, f32[4,1024,256,4]{2,1,3,0:T(8,128)} %get-tuple-element.456, f32[4,4,256]{2,1,0:T(4,128)S(1)} %select_maximum_fusion.4, bf16[1,1024,4,128]{3,2,1,0:T(4,128)(2,1)S(1)} %copy-done.1, f32[4,4,256]{2,1,0:T(4,128)S(1)} %get-tuple-element.459, ...), kind=kOutput, calls=%fused_computation.28.clone.1 | convolution fusion | flops 1087897600 | bytes 22052864 | tf_op jit(solution)/shard_map/while/body/eval_jaxpr/kgrp,pkd->kgrd/dot_general | solution.py:28
  265.8 52.2 %while.44 = (s32[]{:T(128)}, f32[4,4,256]{2,1,0:T(4,128)S(1)}, f32[4,4,256]{2,1,0:T(4,128)S(1)}, f32[4,4,256,128]{3,2,1,0:T(8,128)S(1)}, bf16[2,1024,4,128]{3,1,...) while((s32[]{:T(128)}, f32[4,4,256]{2,1,0:T(4,128)S(1)}, ...), condition=%wide.region_7.8_spmd, body=%wide.region_4.7_spmd.sunk | while | flops 2182094848 | bytes 66323060 | solution.py:49
  266.0 9.3 %bitcast_reduce_fusion.4 = (f32[4,4,256]{2,1,0:T(4,128)S(1)}, f32[4,1024,256,4]{2,1,3,0:T(8,128)}) fusion(bf16[256,4,4,128]{3,0,2,1:T(8,128)(2,1)S(1)} %get-tuple-element.521, bf16[2,1024,4,128]{3,1,2,0:T(8,128)(2,1)} %get-tuple-element.520, s32[]{:T(128)} %get-tuple-element.508), kind=kOutput, calls=%fused_computation.1.clone.1 | convolution fusion | flops 1082126336 | bytes 18891264 | tf_op jit(solution)/shard_map/while/body/eval_jaxpr/rkgd,pkd->kgrp/dot_general | solution.py:19
  275.3 8.7 %fusion.78 = f32[4,4,256]{2,1,0:T(4,128)S(1)} fusion(f32[4,1024,256,4]{2,1,3,0:T(8,128)} %get-tuple-element.444, f32[4,4,256]{2,1,0:T(4,128)S(1)} %max.16), kind=kLoop, calls=%fused_computation.4.clone.1 | loop fusion | flops 12578816 | bytes 16809984 | tf_op jit(solution)/shard_map/while/body/eval_jaxpr/reduce_sum | solution.py:27
  284.1 7.9 %multiply_add_fusion.5 = f32[4,4,256,128]{3,2,1,0:T(8,128)S(1)} fusion(f32[4,4,256,128]{3,2,1,0:T(8,128)S(1)} %get-tuple-element.511, f32[4,1024,256,4]{2,1,3,0:T(8,128)} %get-tuple-element.444, f32[4,4,256]{2,1,0:T(4,128)S(1)} %max.16, bf16[2,1024,4,128]{3,1,2,0:T(8,128)(2,1)S(1)} %copy-done.2, s32[]{:T(128)} %get-tuple-element.508, ...), kind=kOutput, calls=%fused_computation.8.clone.1 | convolution fusion | flops 1087373312 | bytes 22052868 | tf_op jit(solution)/shard_map/while/body/eval_jaxpr/kgrp,pkd->kgrd/dot_general | solution.py:28
  292.0 9.3 %bitcast_reduce_fusion.4 = (f32[4,4,256]{2,1,0:T(4,128)S(1)}, f32[4,1024,256,4]{2,1,3,0:T(8,128)}) fusion(bf16[256,4,4,128]{3,0,2,1:T(8,128)(2,1)S(1)} %get-tuple-element.521, bf16[2,1024,4,128]{3,1,2,0:T(8,128)(2,1)} %get-tuple-element.520, s32[]{:T(128)} %get-tuple-element.508), kind=kOutput, calls=%fused_computation.1.clone.1 | convolution fusion | flops 1082126336 | bytes 18891264 | tf_op jit(solution)/shard_map/while/body/eval_jaxpr/rkgd,pkd->kgrp/dot_general | solution.py:19
  301.3 8.7 %fusion.78 = f32[4,4,256]{2,1,0:T(4,128)S(1)} fusion(f32[4,1024,256,4]{2,1,3,0:T(8,128)} %get-tuple-element.444, f32[4,4,256]{2,1,0:T(4,128)S(1)} %max.16), kind=kLoop, calls=%fused_computation.4.clone.1 | loop fusion | flops 12578816 | bytes 16809984 | tf_op jit(solution)/shard_map/while/body/eval_jaxpr/reduce_sum | solution.py:27
  310.0 7.9 %multiply_add_fusion.5 = f32[4,4,256,128]{3,2,1,0:T(8,128)S(1)} fusion(f32[4,4,256,128]{3,2,1,0:T(8,128)S(1)} %get-tuple-element.511, f32[4,1024,256,4]{2,1,3,0:T(8,128)} %get-tuple-element.444, f32[4,4,256]{2,1,0:T(4,128)S(1)} %max.16, bf16[2,1024,4,128]{3,1,2,0:T(8,128)(2,1)S(1)} %copy-done.2, s32[]{:T(128)} %get-tuple-element.508, ...), kind=kOutput, calls=%fused_computation.8.clone.1 | convolution fusion | flops 1087373312 | bytes 22052868 | tf_op jit(solution)/shard_map/while/body/eval_jaxpr/kgrp,pkd->kgrd/dot_general | solution.py:28
  321.6 11.6 %convolution_convert_fusion = bf16[256,4096]{1,0:T(8,128)(2,1)} fusion(bf16[256,2048]{0,1:T(8,128)(2,1)S(1)} %bitcast.153, bf16[2048,4096]{1,0:T(8,128)(2,1)} %param.17), kind=kOutput, calls=%fused_computation.63 | convolution fusion | flops 4296015872 | bytes 19922944 | tf_op jit(solution)/shard_map/dot_general | solution.py:62
  333.3 30.7 %reduce-scatter.3.cloned.1.call-done = bf16[128,4096]{1,0:T(8,128)(2,1)} async-done(((bf16[256,4096]{1,0:T(8,128)(2,1)}), bf16[128,4096]{1,0:T(8,128)(2,1)}) %reduce-scatter.3.cloned.1.call-update) | async-done | bytes 1048592 | tf_op jit(solution)/shard_map/reduce_scatter | solution.py:111
  (91 shorter events, 123.8 us)
Async XLA Ops:
  7.2 56.2 %all-gather.7.cloned.1.call-start = ((), (), s32[]{:S(2)}) async-start(), calls=%async_computation.3 | async-start | bytes 4456448 | tf_op jit(solution)/shard_map/all_gather | solution.py:97
  7.9 130.5 %all-gather.5.cloned.1.call-start = ((), (), s32[]{:S(2)}) async-start(), calls=%async_computation.2 | async-start | bytes 8912896 | tf_op jit(solution)/shard_map/all_gather | solution.py:91
  8.6 324.6 %reduce-scatter.5.cloned.1.call-start = ((), (), s32[]{:S(2)}) async-start(), calls=%async_computation.5 | async-start | bytes 1572864 | tf_op jit(solution)/shard_map/reduce_scatter | solution.py:117
  88.4 5.8 %copy-start = (f32[4,1024,128,4]{2,1,3,0:T(8,128)S(1)}, f32[4,1024,128,4]{2,1,3,0:T(8,128)}, u32[]{:S(2)}) copy-start(f32[4,1024,128,4]{2,1,3,0:T(8,128)} %get-tuple-element.470) | copy-start | bytes 25165828 | tf_op jit(solution)/shard_map/while
  104.9 5.9 %copy-start = (f32[4,1024,128,4]{2,1,3,0:T(8,128)S(1)}, f32[4,1024,128,4]{2,1,3,0:T(8,128)}, u32[]{:S(2)}) copy-start(f32[4,1024,128,4]{2,1,3,0:T(8,128)} %get-tuple-element.470) | copy-start | bytes 25165828 | tf_op jit(solution)/shard_map/while
  128.9 235.0 %reduce-scatter.3.cloned.1.call-start = ((), (), s32[]{:S(2)}) async-start(), calls=%async_computation.4 | async-start | bytes 3145728 | tf_op jit(solution)/shard_map/reduce_scatter | solution.py:111
  168.2 8.7 %copy-start.1 = (bf16[1,1024,4,128]{3,2,1,0:T(4,128)(2,1)S(1)}, bf16[1,1024,4,128]{3,2,1,0:T(4,128)(2,1)}, u32[]{:S(2)}) copy-start(bf16[1,1024,4,128]{3,2,1,0:T(4,128)(2,1)} %get-tuple-element.458) | copy-start | bytes 3145732 | tf_op jit(solution)/shard_map/while
  195.2 8.7 %copy-start.1 = (bf16[1,1024,4,128]{3,2,1,0:T(4,128)(2,1)S(1)}, bf16[1,1024,4,128]{3,2,1,0:T(4,128)(2,1)}, u32[]{:S(2)}) copy-start(bf16[1,1024,4,128]{3,2,1,0:T(4,128)(2,1)} %get-tuple-element.458) | copy-start | bytes 3145732 | tf_op jit(solution)/shard_map/while
  222.1 8.7 %copy-start.1 = (bf16[1,1024,4,128]{3,2,1,0:T(4,128)(2,1)S(1)}, bf16[1,1024,4,128]{3,2,1,0:T(4,128)(2,1)}, u32[]{:S(2)}) copy-start(bf16[1,1024,4,128]{3,2,1,0:T(4,128)(2,1)} %get-tuple-element.458) | copy-start | bytes 3145732 | tf_op jit(solution)/shard_map/while
  249.1 8.7 %copy-start.1 = (bf16[1,1024,4,128]{3,2,1,0:T(4,128)(2,1)S(1)}, bf16[1,1024,4,128]{3,2,1,0:T(4,128)(2,1)}, u32[]{:S(2)}) copy-start(bf16[1,1024,4,128]{3,2,1,0:T(4,128)(2,1)} %get-tuple-element.458) | copy-start | bytes 3145732 | tf_op jit(solution)/shard_map/while
  275.3 8.7 %copy-start.2 = (bf16[2,1024,4,128]{3,1,2,0:T(8,128)(2,1)S(1)}, bf16[2,1024,4,128]{3,1,2,0:T(8,128)(2,1)}, u32[]{:S(2)}) copy-start(bf16[2,1024,4,128]{3,1,2,0:T(8,128)(2,1)} %get-tuple-element.522) | copy-start | bytes 6291460 | tf_op jit(solution)/shard_map/while
  301.3 8.7 %copy-start.2 = (bf16[2,1024,4,128]{3,1,2,0:T(8,128)(2,1)S(1)}, bf16[2,1024,4,128]{3,1,2,0:T(8,128)(2,1)}, u32[]{:S(2)}) copy-start(bf16[2,1024,4,128]{3,1,2,0:T(8,128)(2,1)} %get-tuple-element.522) | copy-start | bytes 6291460 | tf_op jit(solution)/shard_map/while
Sparse Core Ops, SparseCore 0:
  10.2 53.1 all-gather.6
  65.5 72.8 all-gather.4
  141.2 18.9 reduce-scatter.4
  333.4 30.5 reduce-scatter.2
